TPU v7x, 32 devices: a whole 2x2x4 slice. The times are simulated.
32 devices in a mesh: dp: 8 (over y, x, core), mp: 4 (over z).
Axes of the slice: x: 2, y: 2, z: 4, core: 2. Of those that a mesh axis runs over, the one named last changes fastest.
Arguments:
- ref_hidden: bfloat16 [512, 2048], P('dp', 'mp'), may hold values from -80 to 80
- proxy_hidden: bfloat16 [512, 2048], P('dp', 'mp'), may hold values from -80 to 80
- ref_gain: float32 [2048], replicated, may hold values from 0.5 to 1.5
- proxy_gain: float32 [2048], replicated, may hold values from 0.5 to 1.5
- ref_head: bfloat16 [2048, 128256], P(None, ('dp', 'mp')), may hold values from -16 to 16
- proxy_head: bfloat16 [2048, 128256], P(None, ('dp', 'mp')), may hold values from -16 to 16
- token_ids: int32 [512], P('dp'), may hold values from 0 to 128255
- bucket_ids: int32 [512], P(('dp', 'mp')), may hold values from 0 to 4095
- domain_of_bucket: int32 [4096], replicated, may hold values from 0 to 21
- prior_weights: float32 [22], replicated, may hold values from 0.01 to 0.1
Outputs:
- ref_loss: float32 [512], P(('dp', 'mp'))
- proxy_loss: float32 [512], P(('dp', 'mp'))
- bucket_excess: float32 [4096], P(('dp', 'mp'))
- domain_log_weights: float32 [22], replicated
All inputs are finite; a program needn't handle non-finite values.
Results may differ from a plain program's by a relative error of at most 0.0035.
Values may be sent and summed in bfloat16 or wider, within the bound.
No kernel may reach another device: no remote copies, remote signals or barrier semaphores. Data moves between devices by JAX's collectives and lax.ppermute only.
A program may use at most 128 MiB of HBM per device.

v0:
```python
import jax
import jax.numpy as jnp
from jax import lax
from jax.sharding import PartitionSpec as P


def normalize(hidden, gain):
    values = hidden.astype(jnp.float32)
    scale = lax.rsqrt(jnp.mean(values * values, -1, keepdims=True) + 1e-05)
    return (values * scale * gain).astype(jnp.bfloat16)


def row_stats(normed, targets, head, offset):
    logits = jnp.dot(normed, head, preferred_element_type=jnp.float32)
    top = jnp.max(logits, -1)
    total = jnp.sum(jnp.exp(logits - top[:, None]), -1)
    columns = lax.broadcasted_iota(jnp.int32, logits.shape, 1) + offset
    target = jnp.sum(jnp.where(columns == targets[:, None], logits, 0.0), -1)
    return (top, total, target)


def both_stats(norm_ref, norm_proxy, targets, ref_head, proxy_head, offset):
    first = row_stats(norm_ref, targets, ref_head, offset)
    second = row_stats(norm_proxy, targets, proxy_head, offset)
    return tuple((jnp.stack([left, right]) for left, right in zip(first, second)))


def on_device(
    ref_hidden,
    proxy_hidden,
    ref_gain,
    proxy_gain,
    ref_head,
    proxy_head,
    token_ids,
    bucket_ids,
    domain_of_bucket,
    prior_weights,
):
    vocab_dev = ref_head.shape[1]
    device = lax.axis_index(("dp", "mp"))
    offset = device * vocab_dev
    own_rows = bucket_ids.shape[0]
    full_ref, full_proxy = (
        lax.all_gather(ref_hidden, "mp", axis=1, tiled=True),
        lax.all_gather(proxy_hidden, "mp", axis=1, tiled=True),
    )
    norm_ref = normalize(full_ref, ref_gain)
    norm_proxy = normalize(full_proxy, proxy_gain)
    stats = both_stats(
        lax.all_gather(norm_ref, "dp", axis=0, tiled=True),
        lax.all_gather(norm_proxy, "dp", axis=0, tiled=True),
        lax.all_gather(token_ids, "dp", axis=0, tiled=True),
        ref_head,
        proxy_head,
        offset,
    )
    top, total, target = tuple((fresh for fresh in stats))
    first_row = device * own_rows
    whole_top = lax.pmax(top, ("dp", "mp"))
    terms = jnp.concatenate([total * jnp.exp(top - whole_top), target], 0)
    shares = lax.psum_scatter(terms, ("dp", "mp"), scatter_dimension=1, tiled=True)
    own_top = lax.dynamic_slice_in_dim(whole_top, first_row, own_rows, 1)
    own_total = shares[:2]
    own_target = shares[2:]
    losses = own_top + jnp.log(own_total) - own_target
    excess = jnp.maximum(losses[1] - losses[0], 0.0)
    buckets = domain_of_bucket.shape[0]
    domains = prior_weights.shape[0]
    onehot = (bucket_ids[:, None] == lax.broadcasted_iota(jnp.int32, (1, buckets), 1)).astype(
        jnp.float32
    )
    table = jnp.dot(
        jnp.stack([excess, jnp.ones_like(excess)]),
        onehot,
        precision=lax.Precision.HIGHEST,
        preferred_element_type=jnp.float32,
    )
    domain_hot = (
        domain_of_bucket[:, None] == lax.broadcasted_iota(jnp.int32, (1, domains), 1)
    ).astype(jnp.float32)
    bucket_dev = buckets // lax.axis_size(("dp", "mp"))
    first_bucket = device * bucket_dev
    full_table = lax.psum(table, ("dp", "mp"))
    domain_totals = jnp.dot(
        full_table, domain_hot, precision=lax.Precision.HIGHEST, preferred_element_type=jnp.float32
    )
    own_table = lax.dynamic_slice_in_dim(full_table, first_bucket, bucket_dev, 1)
    bucket_excess = own_table[0] / jnp.maximum(own_table[1], 1.0)
    domain_excess = domain_totals[0] / jnp.maximum(domain_totals[1], 1.0)
    weights = jax.nn.softmax(jnp.log(prior_weights) + 1.0 * domain_excess)
    domain_log_weights = jnp.log(0.999 * weights + 0.001 / domains)
    return (losses[0], losses[1], bucket_excess, domain_log_weights)


def solution(mesh):
    placed = (
        P("dp", "mp"),
        P("dp", "mp"),
        P(),
        P(),
        P(None, ("dp", "mp")),
        P(None, ("dp", "mp")),
        P("dp"),
        P(("dp", "mp")),
        P(),
        P(),
    )
    return jax.shard_map(
        on_device,
        mesh=mesh,
        in_specs=placed,
        out_specs=(P(("dp", "mp")), P(("dp", "mp")), P(("dp", "mp")), P()),
        check_vma=False,
    )
```

profile of v0, /device:TPU:12, one launch (start us, length us, event | category | flops | bytes accessed | tf_op | source)
XLA Modules:
  0.0 333.8 jit_solution(15853292360239945124)
XLA Ops:
  7.2 14.8 %all_gather.17 = bf16[64,2048]{1,0:T(8,128)(2,1)S(1)} all-gather(bf16[64,512]{1,0:T(8,128)(2,1)} %param.11), channel_id=1, replica_groups=mesh['dp'=8,'mp'=4] {'mp'}, dimensions={1}, use_global_device_ids=true | all-gather | bytes 327680 | tf_op jit(solution)/shard_map/all_gather | solution.py:46
  22.2 1.5 fusion.7
  23.8 14.1 %all_gather.15 = bf16[64,2048]{1,0:T(8,128)(2,1)S(1)} all-gather(bf16[64,512]{1,0:T(8,128)(2,1)} %param.10), channel_id=1, replica_groups=mesh['dp'=8,'mp'=4] {'mp'}, dimensions={1}, use_global_device_ids=true | all-gather | bytes 327680 | tf_op jit(solution)/shard_map/all_gather | solution.py:45
  38.1 1.5 fusion.4
  39.7 1.2 dynamic-slice
  41.6 0.9 dynamic-update-slice
  42.4 7.4 %all-reduce.1 = s32[512]{0:T(512)S(1)} all-reduce(s32[512]{0:T(512)S(1)} %dynamic-update-slice), channel_id=1, replica_groups=mesh['dp'=8,'mp'=4] {'dp'}, use_global_device_ids=true, to_apply=%add.1 | all-reduce | flops 512 | bytes 4096
  49.8 3.0 all-gather.5.cloned.1.call-done
  52.8 14.5 %fusion.19 = (f32[512]{0:T(512)S(1)}, f32[512,4008]{0,1:T(8,128)}) fusion(bf16[512,2048]{1,0:T(8,128)(2,1)} %all-gather.5.cloned.1.call-done, bf16[2048,4008]{0,1:T(8,128)(2,1)} %param.15), kind=kOutput, calls=%fused_computation.45 | convolution fusion | flops 8407436800 | bytes 26724352 | tf_op jit(solution)/shard_map/dot_general | solution.py:14
  67.3 15.1 %all-gather.3.cloned.1.call-done = bf16[512,2048]{1,0:T(8,128)(2,1)} async-done(((bf16[64,2048]{1,0:T(8,128)(2,1)}), bf16[512,2048]{1,0:T(8,128)(2,1)}) %all-gather.3.cloned.1.call-update) | async-done | bytes 2097168 | tf_op jit(solution)/shard_map/all_gather | solution.py:51
  82.5 14.4 %fusion.18 = (f32[512]{0:T(512)S(1)}, f32[512,4008]{0,1:T(8,128)}) fusion(bf16[512,2048]{1,0:T(8,128)(2,1)} %all-gather.3.cloned.1.call-done, bf16[2048,4008]{0,1:T(8,128)(2,1)} %param.14), kind=kOutput, calls=%fused_computation.44 | convolution fusion | flops 8407436800 | bytes 26724352 | tf_op jit(solution)/shard_map/dot_general | solution.py:14
  96.8 40.1 %pmax.7 = f32[2,512]{1,0:T(2,128)S(1)} all-reduce(f32[2,512]{1,0:T(2,128)S(1)} %pad_maximum_fusion.1), channel_id=1, replica_groups=mesh['dp'=8,'mp'=4] {'dp','mp'}, use_global_device_ids=true, to_apply=%region_4.5 | all-reduce | flops 1024 | bytes 8192 | tf_op jit(solution)/shard_map/pmax | solution.py:60
  137.0 7.9 %exponential_reduce_fusion.1 = (f32[512]{0:T(512)S(1)}, f32[512]{0:T(512)S(1)}, f32[512]{0:T(512)S(1)}, f32[512]{0:T(512)S(1)}) fusion(f32[512,4008]{0,1:T(8,128)} %get-tuple-element.18, f32[512]{0:T(512)S(1)} %get-tuple-element.17, s32[512]{0:T(512)S(1)} %all-reduce.1, s32[4008]{0:T(1024)S(1)} %iota_add_fusion, f32[512,4008]{0,1:T(8,128)} %get-tuple-element.20, ...), kind=kLoop, calls=%fused_computation.5 | loop fusion | flops 18466816 | bytes 16447136 | tf_op jit(solution)/shard_map/reduce_sum | solution.py:16
  144.9 0.8 copy.14
  145.8 131.7 %reduce-scatter.4.cloned.1.call-done = f32[16,4]{1,0:T(8,128)} async-done(((f32[512,4]{1,0:T(8,128)}), f32[16,4]{1,0:T(8,128)}) %reduce-scatter.4.cloned.1.call-update) | async-done | bytes 272
  277.5 0.8 fusion.17
  278.6 0.5 subtract_maximum_fusion
  279.1 0.3 fusion.9
  279.4 43.2 %psum.7 = f32[2,4096]{1,0:T(2,128)S(1)} all-reduce(f32[2,4096]{1,0:T(2,128)S(1)} %fusion.9), channel_id=1, replica_groups=mesh['dp'=8,'mp'=4] {'dp','mp'}, use_global_device_ids=true, to_apply=%region_10.11 | all-reduce | flops 8192 | bytes 65536 | tf_op jit(solution)/shard_map/psum | solution.py:84
  322.6 0.3 fusion.8
  322.9 0.6 fusion.16
  323.6 1.3 fusion.15
  324.9 1.9 add_log_fusion
  326.8 0.5 fusion.13
  (25 shorter events, 0.8 us)
Async XLA Ops:
  7.2 45.6 %all-gather.5.cloned.1.call-start = ((), (), s32[]{:S(2)}) async-start(), calls=%async_computation.2 | async-start | bytes 2359296 | tf_op jit(solution)/shard_map/all_gather | solution.py:52
  23.8 58.7 %all-gather.3.cloned.1.call-start = ((), (), s32[]{:S(2)}) async-start(), calls=%async_computation.1 | async-start | bytes 2359296 | tf_op jit(solution)/shard_map/all_gather | solution.py:51
  39.6 237.9 %reduce-scatter.4.cloned.1.call-start = ((), (), s32[]{:S(2)}) async-start(), calls=%async_computation.3 | async-start | bytes 270336
  137.0 142.1 %copy-start.2 = (s32[16]{0:T(128)S(1)}, s32[16]{0:T(128)}, u32[]{:S(2)}) copy-start(s32[16]{0:T(128)} %param.17) | copy-start | bytes 196
  137.0 185.6 %copy-start.1 = (s32[4096]{0:T(1024)S(1)}, s32[4096]{0:T(1024)}, u32[]{:S(2)}) copy-start(s32[4096]{0:T(1024)} %param.18) | copy-start | bytes 49156
  137.0 185.9 %copy-start = (f32[22]{0:T(128)S(1)}, f32[22]{0:T(128)}, u32[]{:S(2)}) copy-start(f32[22]{0:T(128)} %param.19) | copy-start | bytes 268
Sparse Core Ops, SparseCore 0:
  23.9 28.8 all-gather.4
  54.7 27.7 all-gather.2
  145.9 131.5 reduce-scatter.3
where the time goes:
time: 335 us; the launch traced here: 334 us
  waiting for transfers between devices  150 us (45%)
  blocking collectives  120 us (36%)
  matrix products  29.5 us (9%)
  other arithmetic  16.3 us (5%)
  between operations  14.5 us (4%)
  local copies, waits for them, and re-layouts  3.97 us (1%)
    unnamed x4, waiting for transfers between devices  132 us
    psum x1, blocking collectives, on_device(): full_table = lax.psum(table, ('dp', 'mp'))  43.2 us
    pmax x1, blocking collectives, on_device(): whole_top = lax.pmax(top, ('dp', 'mp'))  40.1 us
    dot_general x2, matrix products, row_stats(): logits = jnp.dot(normed, head, preferred_element_type=jnp.float32)  28.9 us
    all_gather x1, waiting for transfers between devices, on_device(): lax.all_gather(norm_ref, 'dp', axis=0, tiled=True)  15.1 us
    all_gather x1, blocking collectives, on_device(): lax.all_gather(proxy_hidden, 'mp', axis=1, tiled=True)  14.8 us
    all_gather x1, blocking collectives, on_device(): lax.all_gather(ref_hidden, 'mp', axis=1, tiled=True)  14.1 us
    reduce_sum x1, other arithmetic, row_stats(): total = jnp.sum(jnp.exp(logits - top[:, None]), -1)  7.88 us
  transfers between devices with their start and end apart: 3, of which 3 were waited for; matrix products, arithmetic and copies ran while one was open for 5% of the time, Pallas kernels for 0%

commit v1 on v0

--- a/solution.py
+++ b/solution.py
@@ -2,6 +2,12 @@
 import jax.numpy as jnp
 from jax import lax
 from jax.sharding import PartitionSpec as P
+
+
+def summed_here(x, name):
+    parts = lax.all_gather(x, name, axis=0, tiled=False)
+    total = parts.sum(axis=0)
+    return total
 
 
 def normalize(hidden, gain):
@@ -81,7 +87,7 @@
     ).astype(jnp.float32)
     bucket_dev = buckets // lax.axis_size(("dp", "mp"))
     first_bucket = device * bucket_dev
-    full_table = lax.psum(table, ("dp", "mp"))
+    full_table = summed_here(table, ("dp", "mp"))
     domain_totals = jnp.dot(
         full_table, domain_hot, precision=lax.Precision.HIGHEST, preferred_element_type=jnp.float32
     )

time: 335 us -> 350 us (1.045)
  waiting for transfers between devices: 150 us -> 204 us
  blocking collectives: 120 us -> 76.4 us
    all_gather x0 -> x1, waiting for transfers between devices: none -> 53.8 us  [summed_here(): parts = lax.all_gather(x, name, axis=0, tiled=False)]
    psum x1 -> x0, blocking collectives: 43.2 us -> none  [on_device(): full_table = lax.psum(table, ('dp', 'mp'))]
    unnamed x4 -> x5, waiting for transfers between devices: 132 us -> 132 us
  transfers between devices with their start and end apart: 3 -> 4, of which waited for: 3 -> 4; matrix products, arithmetic and copies ran while one was open for 5% -> 5% of each run, Pallas kernels for 0% -> 0%
where the time goes in v1:
time: 350 us; the launch traced here: 347 us
  waiting for transfers between devices  204 us (58%)
  blocking collectives  76.4 us (22%)
  matrix products  30.1 us (9%)
  other arithmetic  17.8 us (5%)
  between operations  14.5 us (4%)
  local copies, waits for them, and re-layouts  3.97 us (1%)
    unnamed x5, waiting for transfers between devices  132 us
    all_gather x1, waiting for transfers between devices, summed_here(): parts = lax.all_gather(x, name, axis=0, tiled=False)  53.8 us
    pmax x1, blocking collectives, on_device(): whole_top = lax.pmax(top, ('dp', 'mp'))  40.2 us
    dot_general x2, matrix products, row_stats(): logits = jnp.dot(normed, head, preferred_element_type=jnp.float32)  28.9 us
    all_gather x1, waiting for transfers between devices, on_device(): lax.all_gather(norm_ref, 'dp', axis=0, tiled=True)  15.1 us
    all_gather x1, blocking collectives, on_device(): lax.all_gather(proxy_hidden, 'mp', axis=1, tiled=True)  14.8 us
    all_gather x1, blocking collectives, on_device(): lax.all_gather(ref_hidden, 'mp', axis=1, tiled=True)  14.1 us
    reduce_sum x1, other arithmetic, row_stats(): total = jnp.sum(jnp.exp(logits - top[:, None]), -1)  7.88 us
  transfers between devices with their start and end apart: 4, of which 4 were waited for; matrix products, arithmetic and copies ran while one was open for 5% of the time, Pallas kernels for 0%

profile of v1, /device:TPU:12, one launch (start us, length us, event | category | flops | bytes accessed | tf_op | source)
XLA Modules:
  0.0 346.6 jit_solution(574501351042035951)
XLA Ops:
  7.2 14.8 %all_gather.23 = bf16[64,2048]{1,0:T(8,128)(2,1)S(1)} all-gather(bf16[64,512]{1,0:T(8,128)(2,1)} %param.11), channel_id=1, replica_groups=mesh['dp'=8,'mp'=4] {'mp'}, dimensions={1}, use_global_device_ids=true | all-gather | bytes 327680 | tf_op jit(solution)/shard_map/all_gather | solution.py:52
  22.2 1.5 fusion.7
  23.8 14.1 %all_gather.21 = bf16[64,2048]{1,0:T(8,128)(2,1)S(1)} all-gather(bf16[64,512]{1,0:T(8,128)(2,1)} %param.10), channel_id=1, replica_groups=mesh['dp'=8,'mp'=4] {'mp'}, dimensions={1}, use_global_device_ids=true | all-gather | bytes 327680 | tf_op jit(solution)/shard_map/all_gather | solution.py:51
  38.1 1.5 fusion.4
  39.7 1.2 dynamic-slice
  41.6 0.9 dynamic-update-slice
  42.4 7.4 %all-reduce.1 = s32[512]{0:T(512)S(1)} all-reduce(s32[512]{0:T(512)S(1)} %dynamic-update-slice), channel_id=1, replica_groups=mesh['dp'=8,'mp'=4] {'dp'}, use_global_device_ids=true, to_apply=%add.1 | all-reduce | flops 512 | bytes 4096
  49.8 3.0 all-gather.8.cloned.1.call-done
  52.8 14.5 %fusion.18 = (f32[512]{0:T(512)S(1)}, f32[512,4008]{0,1:T(8,128)}) fusion(bf16[512,2048]{1,0:T(8,128)(2,1)} %all-gather.8.cloned.1.call-done, bf16[2048,4008]{0,1:T(8,128)(2,1)} %param.15), kind=kOutput, calls=%fused_computation.45 | convolution fusion | flops 8407436800 | bytes 26724352 | tf_op jit(solution)/shard_map/dot_general | solution.py:20
  67.3 15.1 %all-gather.6.cloned.1.call-done = bf16[512,2048]{1,0:T(8,128)(2,1)} async-done(((bf16[64,2048]{1,0:T(8,128)(2,1)}), bf16[512,2048]{1,0:T(8,128)(2,1)}) %all-gather.6.cloned.1.call-update) | async-done | bytes 2097168 | tf_op jit(solution)/shard_map/all_gather | solution.py:57
  82.5 14.4 %fusion.17 = (f32[512]{0:T(512)S(1)}, f32[512,4008]{0,1:T(8,128)}) fusion(bf16[512,2048]{1,0:T(8,128)(2,1)} %all-gather.6.cloned.1.call-done, bf16[2048,4008]{0,1:T(8,128)(2,1)} %param.14), kind=kOutput, calls=%fused_computation.44 | convolution fusion | flops 8407436800 | bytes 26724352 | tf_op jit(solution)/shard_map/dot_general | solution.py:20
  96.8 40.2 %pmax.7 = f32[2,512]{1,0:T(2,128)S(1)} all-reduce(f32[2,512]{1,0:T(2,128)S(1)} %pad_maximum_fusion.1), channel_id=1, replica_groups=mesh['dp'=8,'mp'=4] {'dp','mp'}, use_global_device_ids=true, to_apply=%region_4.5 | all-reduce | flops 1024 | bytes 8192 | tf_op jit(solution)/shard_map/pmax | solution.py:66
  137.0 7.9 %exponential_reduce_fusion.1 = (f32[512]{0:T(512)S(1)}, f32[512]{0:T(512)S(1)}, f32[512]{0:T(512)S(1)}, f32[512]{0:T(512)S(1)}) fusion(f32[512,4008]{0,1:T(8,128)} %get-tuple-element.18, f32[512]{0:T(512)S(1)} %get-tuple-element.17, s32[512]{0:T(512)S(1)} %all-reduce.1, s32[4008]{0:T(1024)S(1)} %iota_add_fusion, f32[512,4008]{0,1:T(8,128)} %get-tuple-element.20, ...), kind=kLoop, calls=%fused_computation.5 | loop fusion | flops 18466816 | bytes 16447136 | tf_op jit(solution)/shard_map/reduce_sum | solution.py:22
  144.9 0.8 copy.14
  145.9 131.7 %reduce-scatter.4.cloned.1.call-done = f32[16,4]{1,0:T(8,128)} async-done(((f32[512,4]{1,0:T(8,128)}), f32[16,4]{1,0:T(8,128)}) %reduce-scatter.4.cloned.1.call-update) | async-done | bytes 272
  277.5 0.8 fusion.16
  278.6 0.5 subtract_maximum_fusion
  279.1 0.9 convolution_bitcast_fusion
  280.0 53.8 %all-gather.10.cloned.1.call-done = f32[32,2,4096]{2,1,0:T(2,128)} async-done(((f32[1,2,4096]{2,1,0:T(2,128)}), f32[32,2,4096]{2,1,0:T(2,128)}) %all-gather.10.cloned.1.call-update) | async-done | bytes 1048592 | tf_op jit(solution)/shard_map/all_gather | solution.py:8
  333.9 1.5 reduce_sum.78
  335.7 0.6 fusion.15
  336.3 1.3 fusion.14
  337.7 1.9 add_log_fusion
  339.5 0.5 fusion.12
  (28 shorter events, 1.2 us)
Async XLA Ops:
  7.2 45.6 %all-gather.8.cloned.1.call-start = ((), (), s32[]{:S(2)}) async-start(), calls=%async_computation.2 | async-start | bytes 2359296 | tf_op jit(solution)/shard_map/all_gather | solution.py:58
  23.8 58.7 %all-gather.6.cloned.1.call-start = ((), (), s32[]{:S(2)}) async-start(), calls=%async_computation.1 | async-start | bytes 2359296 | tf_op jit(solution)/shard_map/all_gather | solution.py:57
  39.6 237.9 %reduce-scatter.4.cloned.1.call-start = ((), (), s32[]{:S(2)}) async-start(), calls=%async_computation.4 | async-start | bytes 270336
  137.0 142.1 %copy-start.2 = (s32[16]{0:T(128)S(1)}, s32[16]{0:T(128)}, u32[]{:S(2)}) copy-start(s32[16]{0:T(128)} %param.17) | copy-start | bytes 196
  137.0 198.4 %copy-start.1 = (s32[4096]{0:T(1024)S(1)}, s32[4096]{0:T(1024)}, u32[]{:S(2)}) copy-start(s32[4096]{0:T(1024)} %param.18) | copy-start | bytes 49156
  137.0 198.7 %copy-start = (f32[22]{0:T(128)S(1)}, f32[22]{0:T(128)}, u32[]{:S(2)}) copy-start(f32[22]{0:T(128)} %param.19) | copy-start | bytes 268
  145.8 188.0 %all-gather.10.cloned.1.call-start = ((), (), s32[]{:S(2)}) async-start(), calls=%async_computation.3 | async-start | bytes 1081344 | tf_op jit(solution)/shard_map/all_gather | solution.py:8
Sparse Core Ops, SparseCore 0:
  23.9 28.8 all-gather.7
  54.7 27.7 all-gather.5
  145.9 131.5 reduce-scatter.3
  280.4 53.4 all-gather.9
